TPU v7x, 32 devices: a whole 2x2x4 slice. The times are simulated.
32 devices in a mesh: ctx: 8 (over y, x, core), dp: 4 (over z).
Axes of the slice: x: 2, y: 2, z: 4, core: 2. Of those that a mesh axis runs over, the one named last changes fastest.
Arguments:
- ids: int32 [3072], P('ctx'), may hold values from 0 to 511
- embed_table: bfloat16 [512, 4096], P(None, 'dp'), may hold values from -6 to 6
- norm_gain: bfloat16 [4096], P('dp'), may hold values from 0.25 to 1.75
- w_query: bfloat16 [4096, 4096], P('ctx', 'dp'), may hold values from -0.09375 to 0.09375
- w_key: bfloat16 [4096, 4096], P('ctx', 'dp'), may hold values from -0.09375 to 0.09375
- w_value: bfloat16 [4096, 4096], P('ctx', 'dp'), may hold values from -0.09375 to 0.09375
- short_filter: float32 [3, 3, 4096], P(None, None, 'dp'), may hold values from -4 to 4
- pole_rate: float32 [4096, 16], P('dp'), may hold values from 1.6276042e-05 to 0.05
- residue: float32 [4096, 16], P('dp'), may hold values from -2 to 2
- skip_gain: float32 [4096], P('dp'), may hold values from -4 to 4
- w_out: bfloat16 [4096, 4096], P('ctx', 'dp'), may hold values from -0.09375 to 0.09375
Outputs:
- block_out: bfloat16 [3072, 4096], P('ctx', 'dp')
All inputs are finite; a program needn't handle non-finite values.
Results may differ from a plain program's by a relative error of at most 0.0082.
Values may be sent and summed in bfloat16 or wider, within the bound.
A program may use at most 128 MiB of HBM per device.

v0:
```python
import math
import jax
import jax.numpy as jnp
from jax import lax
from jax.sharding import PartitionSpec as P


def shifted(value, axis, steps):
    count = lax.axis_size(axis)
    initial, last = (max(0, -steps), min(count, count - steps))
    return lax.ppermute(value, axis, [(source, source + steps) for source in range(initial, last)])


def entering_2(value, axis, combine, identity):
    peers, index = (lax.axis_size(axis), lax.axis_index(axis))
    everything = jax.tree.map(lambda part: lax.all_gather(part, axis), value)
    start = jax.tree.map(
        lambda part, zero: jnp.broadcast_to(jnp.asarray(zero, part.dtype), part.shape),
        value,
        identity,
    )

    def turn(k, before):
        reached = k < index
        new = combine(before, jax.tree.map(lambda part: part[k], everything))
        return jax.tree.map(lambda a, b: jnp.where(reached, a, b), new, before)

    return lax.fori_loop(0, peers, turn, start)


def shards(
    ids,
    embed_table,
    norm_gain,
    w_query,
    w_key,
    w_value,
    short_filter,
    pole_rate,
    residue,
    skip_gain,
    w_out,
):
    highest = lax.Precision.HIGHEST
    vocab = embed_table.shape[0]
    channels = w_query.shape[1]
    one_hot = (ids[:, None] == jnp.arange(vocab, dtype=jnp.int32)[None, :]).astype(jnp.bfloat16)
    embedded = jnp.dot(one_hot, embed_table, preferred_element_type=jnp.float32).astype(
        jnp.bfloat16
    )
    full_rows, full_gain = (
        lax.all_gather(embedded, "dp", axis=1, tiled=True),
        lax.all_gather(norm_gain, "dp", axis=0, tiled=True),
    )
    floated = full_rows.astype(jnp.float32)
    scale = lax.rsqrt(jnp.mean(floated * floated, axis=1, keepdims=True) + 1e-06)
    normed = (floated * scale * full_gain.astype(jnp.float32)[None, :]).astype(jnp.bfloat16)
    tok_rows = normed.shape[0]

    def add_rows(piece):
        return jnp.dot(normed, piece, preferred_element_type=jnp.float32)

    query_proj = add_rows(lax.all_gather(w_query, "ctx", axis=0, tiled=True))
    key_proj = add_rows(lax.all_gather(w_key, "ctx", axis=0, tiled=True))
    value_proj = add_rows(lax.all_gather(w_value, "ctx", axis=0, tiled=True))
    projected = jnp.concatenate([query_proj, key_proj, value_proj], axis=1).astype(jnp.bfloat16)
    taps = short_filter.shape[0]
    previous = shifted(projected[tok_rows - (taps - 1) :], "ctx", 1)
    extended = jnp.concatenate([previous, projected], axis=0).astype(jnp.float32)
    filt_rows = short_filter.reshape(taps, 3 * channels)
    convolved = jnp.zeros((tok_rows, 3 * channels), jnp.float32)
    for tap in range(taps):
        convolved = (
            convolved
            + filt_rows[tap][None, :] * extended[taps - 1 - tap : taps - 1 - tap + tok_rows]
        )
    query_conv = convolved[:, :channels]
    gated = convolved[:, channels : 2 * channels] * convolved[:, 2 * channels :]
    sub_len = math.gcd(tok_rows, 64)
    blocks = tok_rows // sub_len
    lag_index = jnp.arange(sub_len, dtype=jnp.int32)
    lags = lag_index.astype(jnp.float32)
    strength = residue * jnp.sqrt(2.0 * pole_rate)
    kernel = jnp.einsum(
        "lck,ck->lc", jnp.exp(-pole_rate[None] * lags[:, None, None]), strength, precision=highest
    )
    offsets = lag_index[:, None] - lag_index[None, :]
    toeplitz = jnp.where((offsets >= 0)[:, :, None], kernel[jnp.maximum(offsets, 0)], 0.0)
    pieces = gated.reshape(blocks, sub_len, channels)
    inside = jnp.einsum("tsc,bsc->btc", toeplitz, pieces, precision=highest)
    tail_decay = jnp.exp(-pole_rate[None] * (sub_len - 1.0 - lags)[:, None, None])
    block_ends = jnp.einsum("sck,bsc->bck", tail_decay, pieces, precision=highest)
    step_decay = jnp.exp(-pole_rate * float(sub_len))

    def advance(state, block_end):
        return (step_decay * state + block_end, state)

    device_end, entering = lax.scan(advance, jnp.zeros_like(step_decay), block_ends)
    device_decay = jnp.exp(-pole_rate * float(tok_rows))

    def combine(earlier, later):
        return (earlier[0] * later[0], later[0] * earlier[1] + later[1])

    decay_total, incoming = entering_2(
        (device_decay, device_end),
        "ctx",
        combine,
        (jnp.ones_like(device_decay), jnp.zeros_like(device_end)),
    )
    block_pos = jnp.arange(blocks, dtype=jnp.float32) * float(sub_len)
    states_in = entering + jnp.exp(-pole_rate[None] * block_pos[:, None, None]) * incoming[None]
    lead = jnp.exp(-pole_rate[None] * (lags + 1.0)[:, None, None]) * strength[None]
    carried = jnp.einsum("tck,bck->btc", lead, states_in, precision=highest)
    long_conv = (inside + carried).reshape(tok_rows, channels) + skip_gain[None, :] * gated
    mixed = (query_conv * long_conv).astype(jnp.bfloat16)
    all_mixed = lax.all_gather(mixed, "dp", axis=1, tiled=True)
    output = jnp.dot(
        all_mixed,
        lax.all_gather(w_out, "ctx", axis=0, tiled=True),
        preferred_element_type=jnp.float32,
    )
    return (embedded.astype(jnp.float32) + output).astype(jnp.bfloat16)


def solution(mesh):
    placed = (
        P("ctx"),
        P(None, "dp"),
        P("dp"),
        P("ctx", "dp"),
        P("ctx", "dp"),
        P("ctx", "dp"),
        P(None, None, "dp"),
        P("dp", None),
        P("dp", None),
        P("dp"),
        P("ctx", "dp"),
    )
    return jax.shard_map(
        shards, mesh=mesh, in_specs=placed, out_specs=P("ctx", "dp"), check_vma=False
    )
```

profile of v0, /device:TPU:0, one launch (start us, length us, event | category | flops | bytes accessed | tf_op | source)
XLA Modules:
  0.0 511.5 jit_solution(16965274444478616923)
XLA Ops:
  6.6 1.2 copy-done
  7.8 2.2 convolution_convert_fusion.3
  13.3 12.5 %multiply_reduce_fusion = f32[1024,64]{1,0:T(8,128)} fusion(f32[1024,16]{1,0:T(8,128)S(1)} %copy.47, f32[64]{0:T(128)S(1)} %iota_convert_fusion, f32[1024,16]{1,0:T(8,128)S(1)} %copy.30), kind=kLoop, calls=%fused_computation.14 | loop fusion | flops 3080192 | bytes 393472
  25.9 14.8 %all_gather.34 = bf16[4096]{0:T(1024)(128)(2,1)S(1)} all-gather(bf16[1024]{0:T(1024)(128)(2,1)S(1)} %copy-done.12), channel_id=1, replica_groups=mesh['ctx'=8,'dp'=4] {'dp'}, dimensions={0}, use_global_device_ids=true | all-gather | bytes 10240 | tf_op jit(solution)/shard_map/all_gather | solution.py:53
  40.7 10.9 %all-gather = f32[8192,16]{0,1:T(8,128)} all-gather(f32[1024,16]{0,1:T(8,128)S(1)} %get-tuple-element.213), channel_id=2, replica_groups=mesh['ctx'=8,'dp'=4] {'ctx'}, dimensions={0}, use_global_device_ids=true | all-gather | bytes 589824 | tf_op jit(solution)/shard_map/all_gather | solution.py:16
  51.6 24.7 %all-gather.9.cloned.1.call-done = bf16[384,4096]{1,0:T(8,128)(2,1)} async-done(((bf16[384,1024]{1,0:T(8,128)(2,1)}), bf16[384,4096]{1,0:T(8,128)(2,1)}) %all-gather.9.cloned.1.call-update) | async-done | bytes 3145744 | tf_op jit(solution)/shard_map/all_gather | solution.py:52
  76.3 2.6 fusion.14
  78.9 52.2 %all-gather.15.cloned.1.call-done = bf16[4096,1024]{1,0:T(8,128)(2,1)} async-done(((bf16[512,1024]{1,0:T(8,128)(2,1)}), bf16[4096,1024]{1,0:T(8,128)(2,1)}) %all-gather.15.cloned.1.call-update) | async-done | bytes 8388624 | tf_op jit(solution)/shard_map/all_gather | solution.py:65
  131.2 7.8 %convolution_convert_fusion = bf16[384,1024]{1,0:T(8,128)(2,1)S(1)} fusion(bf16[4096,1024]{1,0:T(8,128)(2,1)} %all-gather.15.cloned.1.call-done, bf16[384,4096]{1,0:T(8,128)(2,1)} %all-gather.9.cloned.1.call-done, f32[4096]{0:T(1024)S(1)} %convert_element_type.46, f32[384]{0:T(512)S(1)} %add_rsqrt_fusion), kind=kOutput, calls=%fused_computation.45 | convolution fusion | flops 3227910144 | bytes 12338688 | tf_op jit(solution)/shard_map/dot_general | solution.py:61
  139.0 48.4 %all-gather.13.cloned.1.call-done = bf16[4096,1024]{1,0:T(8,128)(2,1)} async-done(((bf16[512,1024]{1,0:T(8,128)(2,1)}), bf16[4096,1024]{1,0:T(8,128)(2,1)}) %all-gather.13.cloned.1.call-update) | async-done | bytes 8388624 | tf_op jit(solution)/shard_map/all_gather | solution.py:64
  187.3 7.8 %convolution_convert_fusion.1 = bf16[384,1024]{1,0:T(8,128)(2,1)S(1)} fusion(bf16[4096,1024]{1,0:T(8,128)(2,1)} %all-gather.13.cloned.1.call-done, bf16[384,4096]{1,0:T(8,128)(2,1)} %all-gather.9.cloned.1.call-done, f32[4096]{0:T(1024)S(1)} %convert_element_type.46, f32[384]{0:T(512)S(1)} %add_rsqrt_fusion), kind=kOutput, calls=%fused_computation.46 | convolution fusion | flops 3227910144 | bytes 12338688 | tf_op jit(solution)/shard_map/dot_general | solution.py:61
  195.1 48.2 %all-gather.11.cloned.1.call-done = bf16[4096,1024]{1,0:T(8,128)(2,1)} async-done(((bf16[512,1024]{1,0:T(8,128)(2,1)}), bf16[4096,1024]{1,0:T(8,128)(2,1)}) %all-gather.11.cloned.1.call-update) | async-done | bytes 8388624 | tf_op jit(solution)/shard_map/all_gather | solution.py:63
  243.4 7.8 %convolution_convert_fusion.2 = bf16[384,1024]{1,0:T(8,128)(2,1)S(1)} fusion(bf16[4096,1024]{1,0:T(8,128)(2,1)} %all-gather.11.cloned.1.call-done, bf16[384,4096]{1,0:T(8,128)(2,1)} %all-gather.9.cloned.1.call-done, f32[4096]{0:T(1024)S(1)} %convert_element_type.46, f32[384]{0:T(512)S(1)} %add_rsqrt_fusion), kind=kOutput, calls=%fused_computation.47 | convolution fusion | flops 3227910144 | bytes 12338688 | tf_op jit(solution)/shard_map/dot_general | solution.py:61
  251.2 2.2 collective-permute-start
  253.5 1.2 copy.44
  254.7 18.9 %gather_fusion = f32[4096,1024]{1,0:T(8,128)} fusion(f32[64,1024]{1,0:T(8,128)S(1)} %bitcast.57, s32[4096]{0:T(1024)S(1)} %broadcast_clamp_fusion), kind=kCustom, calls=%fused_computation | custom fusion | bytes 33570816 | tf_op jit(solution)/shard_map/gather | solution.py:88
  273.6 30.7 %copy.31 = f32[64,64,1024]{1,0,2:T(8,128)} copy(f32[64,64,1024]{2,1,0:T(8,128)} %bitcast.58) | data formatting | bytes 33554432 | tf_op jit(solution)/shard_map/gather | solution.py:88
  304.3 2.1 copy.48
  307.2 1.4 fusion.17
  308.6 2.2 copy-done.2
  311.1 2.7 copy.32
  313.8 16.9 %fusion.24 = f32[6,1024,16]{2,0,1:T(8,128)} fusion(f32[6,64,1024]{1,0,2:T(8,128)} %copy.32, f32[64]{0:T(128)S(1)} %broadcast_subtract_fusion, f32[1024,16]{1,0:T(8,128)S(1)} %copy.30), kind=kOutput, calls=%fused_computation.39 | convolution fusion | flops 76546048 | bytes 2031872 | tf_op jit(solution)/shard_map/sck,bsc->bck/dot_general | solution.py:92
  330.7 2.7 copy.34
  333.8 10.3 %all-gather.1 = f32[8192,16]{0,1:T(8,128)S(1)} all-gather(f32[1024,16]{0,1:T(8,128)S(1)} %get-tuple-element.128), channel_id=3, replica_groups=mesh['ctx'=8,'dp'=4] {'ctx'}, dimensions={0}, use_global_device_ids=true | all-gather | bytes 589824 | tf_op jit(solution)/shard_map/all_gather | solution.py:16
  344.3 9.8 %while.28 = (s32[]{:T(128)}, f32[1024,16]{0,1:T(8,128)S(1)}, s32[]{:T(128)}, f32[8,1024,16]{1,0,2:T(8,128)}, f32[8,1024,16]{1,0,2:T(8,128)S(1)}, /*index=5*/s32[]{:T(128)}, s32[]{:T(128)}) while((s32[]{:T(128)}, f32[1024,16]{0,1:T(8,128)S(1)}, s32[]{:T(128)}, f32[8,1024,16]{1,0,2:T(8,128)}, f32[8,1024,16]{1,0,2:T(8,128)S(1)}, ...), condition=%wide.region_4.5_spmd.clone, body=%wide.region_3.4_spmd.clone.sunk | while | flops 65540 | bytes 524397 | solution.py:28
  354.2 2.7 copy.38
  356.9 56.2 %fusion.3 = f32[1024,6,64]{2,1,0:T(8,128)S(1)} fusion(f32[6,64,1024]{1,0,2:T(8,128)} %copy.32, f32[64,64,1024]{1,0,2:T(8,128)} %copy.31, pred[64,64]{1,0:T(8,128)(4,1)S(1)} %subtract_compare_fusion), kind=kOutput, calls=%fused_computation.10 | convolution fusion | flops 306184192 | bytes 19927040 | tf_op jit(solution)/shard_map/tsc,bsc->btc/dot_general | solution.py:90
  413.2 12.3 %add_bitcast_fusion = f32[6,64,1024]{1,0,2:T(8,128)} fusion(f32[1024,6,64]{2,1,0:T(8,128)S(1)} %fusion.3, f32[6,1024,16]{2,0,1:T(8,128)S(1)} %copy-done.3, f32[1024,16]{1,0:T(8,128)S(1)} %copy-done.6, f32[64]{0:T(128)S(1)} %broadcast_add_fusion, f32[1024,16]{1,0:T(8,128)S(1)} %copy.30), kind=kOutput, calls=%fused_computation.32 | convolution fusion | flops 77987840 | bytes 3670272 | tf_op jit(solution)/shard_map/tck,bck->btc/dot_general | solution.py:113
  425.5 2.7 copy.39
  428.2 3.9 fusion.29
  432.2 63.5 %all-gather.17.cloned.1.call-done = bf16[384,4096]{1,0:T(8,128)(2,1)} async-done(((bf16[384,1024]{1,0:T(8,128)(2,1)}), bf16[384,4096]{1,0:T(8,128)(2,1)}) %all-gather.17.cloned.1.call-update) | async-done | bytes 3145744 | tf_op jit(solution)/shard_map/all_gather | solution.py:116
  495.8 8.7 %add_convert_fusion = bf16[384,1024]{1,0:T(8,128)(2,1)} fusion(bf16[384,1024]{1,0:T(8,128)(2,1)S(1)} %copy-done.4, bf16[384,4096]{1,0:T(8,128)(2,1)} %all-gather.17.cloned.1.call-done, bf16[4096,1024]{1,0:T(8,128)(2,1)} %all-gather.19.cloned.1.call-done), kind=kOutput, calls=%fused_computation.44 | convolution fusion | flops 3222405120 | bytes 13107200 | tf_op jit(solution)/shard_map/dot_general | solution.py:117
  (92 shorter events, 14.9 us)
Async XLA Ops:
  6.5 1.2 copy-start
  6.5 6.2 %copy-start.10 = (f32[3,3,1024]{2,1,0:T(4,128)S(1)}, f32[3,3,1024]{2,1,0:T(4,128)}, u32[]{:S(2)}) copy-start(f32[3,3,1024]{2,1,0:T(4,128)} %param.21) | copy-start | bytes 110596
  6.5 6.2 %copy-start.8 = (f32[1024,16]{0,1:T(8,128)S(1)}, f32[1024,16]{0,1:T(8,128)}, u32[]{:S(2)}) copy-start(f32[1024,16]{0,1:T(8,128)} %param.22) | copy-start | bytes 196612
  6.5 6.2 %copy-start.9 = (f32[1024,16]{0,1:T(8,128)S(1)}, f32[1024,16]{0,1:T(8,128)}, u32[]{:S(2)}) copy-start(f32[1024,16]{0,1:T(8,128)} %param.23) | copy-start | bytes 196612
  6.5 69.8 %all-gather.9.cloned.1.call-start = ((), (), s32[]{:S(2)}) async-start(), calls=%async_computation | async-start | bytes 3932160 | tf_op jit(solution)/shard_map/all_gather | solution.py:52
  9.9 15.9 %copy-start.12 = (bf16[1024]{0:T(1024)(128)(2,1)S(1)}, bf16[1024]{0:T(1024)(128)(2,1)}, u32[]{:S(2)}) copy-start(bf16[1024]{0:T(1024)(128)(2,1)} %param.17) | copy-start | bytes 6148
  10.0 121.2 %all-gather.15.cloned.1.call-start = ((), (), s32[]{:S(2)}) async-start(), calls=%async_computation.3 | async-start | bytes 9437184 | tf_op jit(solution)/shard_map/all_gather | solution.py:65
  10.7 176.6 %all-gather.13.cloned.1.call-start = ((), (), s32[]{:S(2)}) async-start(), calls=%async_computation.2 | async-start | bytes 9437184 | tf_op jit(solution)/shard_map/all_gather | solution.py:64
  11.5 231.9 %all-gather.11.cloned.1.call-start = ((), (), s32[]{:S(2)}) async-start(), calls=%async_computation.1 | async-start | bytes 9437184 | tf_op jit(solution)/shard_map/all_gather | solution.py:63
  12.0 420.2 %all-gather.19.cloned.1.call-start = ((), (), s32[]{:S(2)}) async-start(), calls=%async_computation.5 | async-start | bytes 9437184 | tf_op jit(solution)/shard_map/all_gather | solution.py:119
  12.6 483.1 %all-gather.17.cloned.1.call-start = ((), (), s32[]{:S(2)}) async-start(), calls=%async_computation.4 | async-start | bytes 3932160 | tf_op jit(solution)/shard_map/all_gather | solution.py:116
  13.0 65.9 %copy-start.5 = (f32[1024,16]{1,0:T(8,128)}, f32[1024,16]{1,0:T(8,128)S(1)}, u32[]{:S(2)}) copy-start(f32[1024,16]{1,0:T(8,128)S(1)} %copy.47) | copy-start | bytes 196612
  251.2 55.3 %collective-permute-start = (bf16[2,3072]{1,0:T(2,128)(2,1)S(1)}, bf16[2,3072]{1,0:T(2,128)(2,1)S(1)}, u32[]{:S(2)}, u32[]{:S(2)}) collective-permute-start(bf16[2,3072]{1,0:T(2,128)(2,1)S(1)} %pad_maximum_fusion), channel_id=1, source_target_pairs={{0,4},{4,8},{8,12},{12,16},{16,20},{20,24},{24,28},{1,5},{5,9},{9,... | collective-permute-start | bytes 36872 | tf_op jit(solution)/shard_map/ppermute | solution.py:11
  308.6 2.2 copy-start.2
  313.8 19.5 %copy-start.7 = (f32[6,1024,16]{1,2,0:T(8,128)S(1)}, f32[6,1024,16]{1,2,0:T(8,128)}, u32[]{:S(2)}) copy-start(f32[6,1024,16]{1,2,0:T(8,128)} %custom-call.4) | copy-start | bytes 1179652
  356.9 56.2 %copy-start.3 = (f32[6,1024,16]{2,0,1:T(8,128)S(1)}, f32[6,1024,16]{2,0,1:T(8,128)}, u32[]{:S(2)}) copy-start(f32[6,1024,16]{2,0,1:T(8,128)} %copy.38) | copy-start | bytes 1179652
  356.9 56.2 %copy-start.6 = (f32[1024,16]{1,0:T(8,128)S(1)}, f32[1024,16]{1,0:T(8,128)}, u32[]{:S(2)}) copy-start(f32[1024,16]{1,0:T(8,128)} %copy-done.5) | copy-start | bytes 196612
  425.5 2.7 copy-start.11
  428.2 67.5 %copy-start.4 = (bf16[384,1024]{1,0:T(8,128)(2,1)S(1)}, bf16[384,1024]{1,0:T(8,128)(2,1)}, u32[]{:S(2)}) copy-start(bf16[384,1024]{1,0:T(8,128)(2,1)} %convolution_convert_fusion.3) | copy-start | bytes 2359300
  495.8 8.7 %copy-start.1 = (bf16[512,1024]{1,0:T(8,128)(2,1)S(1)}, bf16[512,1024]{1,0:T(8,128)(2,1)}, u32[]{:S(2)}) copy-start(bf16[512,1024]{1,0:T(8,128)(2,1)} %param.16) | copy-start | bytes 3145732
Sparse Core Ops, SparseCore 0:
  10.1 66.2 all-gather.8
  78.2 52.8 all-gather.14
  133.0 54.2 all-gather.12
  189.1 54.2 all-gather.10
  245.1 54.2 all-gather.18
  432.3 63.4 all-gather.16
where the time goes:
time: 521 us; the launch traced here: 512 us
  waiting for transfers between devices  240 us (46%)
  matrix products  120 us (23%)
  local copies, waits for them, and re-layouts  77.3 us (15%)
  blocking collectives  36 us (7%)
  other arithmetic  22.2 us (4%)
  between operations  14 us (3%)
    all_gather x1, waiting for transfers between devices, shards(): all_mixed = lax.all_gather(mixed, 'dp', axis=1, tiled=True)  63.5 us
    dot_general x1, matrix products, shards(): inside = jnp.einsum('tsc,bsc->btc', toeplitz, pieces, precision=highest)  56.2 us
    all_gather x1, waiting for transfers between devices, shards(): value_proj = add_rows(lax.all_gather(w_value, 'ctx', axis=0, tiled=True))  52.2 us
    gather x2, local copies, waits for them, and re-layouts, shards(): kernel[jnp.maximum(offsets, 0)]  49.6 us
    all_gather x1, waiting for transfers between devices, shards(): key_proj = add_rows(lax.all_gather(w_key, 'ctx', axis=0, tiled=True))  48.4 us
    all_gather x1, waiting for transfers between devices, shards(): query_proj = add_rows(lax.all_gather(w_query, 'ctx', axis=0, tiled=True))  48.2 us
    all_gather x1, waiting for transfers between devices, shards(): lax.all_gather(embedded, 'dp', axis=1, tiled=True)  24.7 us
    dot_general x3, matrix products, add_rows(): return jnp.dot(normed, piece, preferred_element_type=jnp.float32)  23.4 us
  transfers between devices with their start and end apart: 7, of which 5 were waited for; matrix products, arithmetic and copies ran while one was open for 40% of the time, Pallas kernels for 0%

commit v1 on v0

--- a/solution.py
+++ b/solution.py
@@ -1,8 +1,27 @@
+import functools
 import math
 import jax
 import jax.numpy as jnp
 from jax import lax
 from jax.sharding import PartitionSpec as P
+
+
+def change_tasks_for(array_in, comm_axis):
+    then = lax.axis_size(comm_axis)
+    carry_in = lax.axis_index(comm_axis)
+    z2, oldest, t1 = (then, carry_in, array_in.shape[0])
+    frames = [(tick, (tick + 1) % z2) for tick in range(z2)]
+    y_new = jnp.zeros((*array_in.shape[:0], z2 * t1, *array_in.shape[1:]), array_in.dtype)
+    q_next = array_in
+    for i0 in tuple(range(z2)):
+        item_now = (oldest - i0) % z2
+        y_new = lax.dynamic_update_slice_in_dim(y_new, q_next, item_now * t1, axis=0)
+        if i0 < z2 - 1:
+            q_next = lax.ppermute(q_next, comm_axis, frames)
+    return y_new
+
+
+perform_indices = functools.partial(change_tasks_for, comm_axis="ctx")
 
 
 def shifted(value, axis, steps):
@@ -60,7 +79,7 @@
     def add_rows(piece):
         return jnp.dot(normed, piece, preferred_element_type=jnp.float32)
 
-    query_proj = add_rows(lax.all_gather(w_query, "ctx", axis=0, tiled=True))
+    query_proj = add_rows(perform_indices(w_query))
     key_proj = add_rows(lax.all_gather(w_key, "ctx", axis=0, tiled=True))
     value_proj = add_rows(lax.all_gather(w_value, "ctx", axis=0, tiled=True))
     projected = jnp.concatenate([query_proj, key_proj, value_proj], axis=1).astype(jnp.bfloat16)

time: 521 us -> 477 us (0.916)
  waiting for transfers between devices: 240 us -> 160 us
  local copies, waits for them, and re-layouts: 77.3 us -> 97.3 us
  blocking collectives: 36 us -> 50.1 us
    ppermute x0 -> x7, waiting for transfers between devices: none -> 64.6 us  [change_tasks_for(): q_next = lax.ppermute(q_next, comm_axis, frames)]
    all_gather x1, waiting for transfers between devices: 52.2 us -> 0.02 us  [shards(): value_proj = add_rows(lax.all_gather(w_value, 'ctx', axis=0, tiled=True))]
    all_gather x1 -> x0, waiting for transfers between devices: 48.2 us -> none  [shards(): query_proj = add_rows(lax.all_gather(w_query, 'ctx', axis=0, tiled=True))]
    all_gather x1, waiting for transfers between devices: 24.7 us -> 0.01 us  [shards(): lax.all_gather(embedded, 'dp', axis=1, tiled=True)]
    all_gather x1, waiting for transfers between devices: 48.4 us -> 30.5 us  [shards(): key_proj = add_rows(lax.all_gather(w_key, 'ctx', axis=0, tiled=True))]
    all_gather x2, blocking collectives: 21.1 us -> 37.6 us  [entering_2(): everything = jax.tree.map(lambda part: lax.all_gather(part, axis), value)]
    dynamic_update_slice x0 -> x8, local copies, waits for them, and re-layouts: none -> 15 us  [change_tasks_for(): lax.dynamic_update_slice_in_dim(y_new, q_next, item_now * t1, axis=0)]
  transfers between devices with their start and end apart: 7 -> 13, of which waited for: 5 -> 7; matrix products, arithmetic and copies ran while one was open for 40% -> 48% of each run, Pallas kernels for 0% -> 0%
where the time goes in v1:
time: 477 us; the launch traced here: 471 us
  waiting for transfers between devices  160 us (34%)
  matrix products  118 us (25%)
  local copies, waits for them, and re-layouts  97.3 us (20%)
  blocking collectives  50.1 us (11%)
  other arithmetic  25.8 us (5%)
  between operations  13.9 us (3%)
  starting transfers between devices  5.41 us (1%)
    ppermute x7, waiting for transfers between devices, change_tasks_for(): q_next = lax.ppermute(q_next, comm_axis, frames)  64.6 us
    all_gather x1, waiting for transfers between devices, shards(): all_mixed = lax.all_gather(mixed, 'dp', axis=1, tiled=True)  63.6 us
    dot_general x1, matrix products, shards(): inside = jnp.einsum('tsc,bsc->btc', toeplitz, pieces, precision=highest)  56.2 us
    gather x2, local copies, waits for them, and re-layouts, shards(): kernel[jnp.maximum(offsets, 0)]  49.5 us
    all_gather x2, blocking collectives, entering_2(): everything = jax.tree.map(lambda part: lax.all_gather(part, axis), value)  37.6 us
    all_gather x1, waiting for transfers between devices, shards(): key_proj = add_rows(lax.all_gather(w_key, 'ctx', axis=0, tiled=True))  30.5 us
    dot_general x3, matrix products, add_rows(): return jnp.dot(normed, piece, preferred_element_type=jnp.float32)  21.7 us
    dot_general x1, matrix products, shards(): jnp.einsum('sck,bsc->bck', tail_decay, pieces, precision=highest)  16.8 us
  transfers between devices with their start and end apart: 13, of which 7 were waited for; matrix products, arithmetic and copies ran while one was open for 48% of the time, Pallas kernels for 0%

profile of v1, /device:TPU:0, one launch (start us, length us, event | category | flops | bytes accessed | tf_op | source)
XLA Modules:
  0.0 471.0 jit_solution(14489906686665083404)
XLA Ops:
  12.1 15.6 %collective-permute-done = bf16[512,1024]{1,0:T(8,128)(2,1)S(1)} collective-permute-done((bf16[512,1024]{1,0:T(8,128)(2,1)}, bf16[512,1024]{1,0:T(8,128)(2,1)S(1)}, u32[]{:S(2)}, u32[]{:S(2)}) %collective-permute-start) | collective-permute-done | bytes 1048608 | tf_op jit(solution)/shard_map/ppermute | solution.py:20
  27.6 15.1 %collective-permute-done.1 = bf16[512,1024]{1,0:T(8,128)(2,1)S(1)} collective-permute-done((bf16[512,1024]{1,0:T(8,128)(2,1)S(1)}, bf16[512,1024]{1,0:T(8,128)(2,1)S(1)}, u32[]{:S(2)}, u32[]{:S(2)}) %collective-permute-start.1) | collective-permute-done | bytes 1048608 | tf_op jit(solution)/shard_map/ppermute | solution.py:20
  42.8 15.1 %collective-permute-done.2 = bf16[512,1024]{1,0:T(8,128)(2,1)S(1)} collective-permute-done((bf16[512,1024]{1,0:T(8,128)(2,1)S(1)}, bf16[512,1024]{1,0:T(8,128)(2,1)S(1)}, u32[]{:S(2)}, u32[]{:S(2)}) %collective-permute-start.2) | collective-permute-done | bytes 1048608 | tf_op jit(solution)/shard_map/ppermute | solution.py:20
  58.2 14.9 %collective-permute-done.3 = bf16[512,1024]{1,0:T(8,128)(2,1)} collective-permute-done((bf16[512,1024]{1,0:T(8,128)(2,1)S(1)}, bf16[512,1024]{1,0:T(8,128)(2,1)}, u32[]{:S(2)}, u32[]{:S(2)}) %collective-permute-start.3) | collective-permute-done | bytes 1048608 | tf_op jit(solution)/shard_map/ppermute | solution.py:20
  73.2 27.4 %all-gather = f32[8192,16]{0,1:T(8,128)} all-gather(f32[1024,16]{0,1:T(8,128)S(1)} %get-tuple-element.213), channel_id=2, replica_groups=mesh['ctx'=8,'dp'=4] {'ctx'}, dimensions={0}, use_global_device_ids=true | all-gather | bytes 589824 | tf_op jit(solution)/shard_map/all_gather | solution.py:35
  100.6 4.3 broadcast_in_dim.15
  106.2 12.5 %all_gather.31 = bf16[4096]{0:T(1024)(128)(2,1)S(1)} all-gather(bf16[1024]{0:T(1024)(128)(2,1)S(1)} %copy-done.15), channel_id=1, replica_groups=mesh['ctx'=8,'dp'=4] {'dp'}, dimensions={0}, use_global_device_ids=true | all-gather | bytes 10240 | tf_op jit(solution)/shard_map/all_gather | solution.py:72
  120.0 16.1 %multiply_reduce_fusion = f32[1024,64]{1,0:T(8,128)} fusion(f32[1024,16]{1,0:T(8,128)} %copy.47, f32[64]{0:T(128)S(1)} %iota_convert_fusion, f32[1024,16]{1,0:T(8,128)S(1)} %copy.30), kind=kLoop, calls=%fused_computation.14 | loop fusion | flops 3080192 | bytes 393472
  136.1 2.4 constant_dynamic-update-slice_fusion.6
  140.8 2.3 collective-permute-start.6
  144.1 2.4 constant_dynamic-update-slice_fusion.3
  146.6 2.7 fusion.14
  152.7 3.8 collective-permute-done.6
  156.5 2.5 constant_dynamic-update-slice_fusion
  159.0 6.1 %convolution_convert_fusion.2 = bf16[384,1024]{1,0:T(8,128)(2,1)S(1)} fusion(bf16[4096,1024]{1,0:T(8,128)(2,1)} %constant_dynamic-update-slice_fusion, bf16[384,4096]{1,0:T(8,128)(2,1)S(1)} %copy-done.4, f32[4096]{0:T(1024)S(1)} %convert_element_type.46, f32[384]{0:T(512)S(1)} %add_rsqrt_fusion), kind=kOutput, calls=%fused_computation.47 | convolution fusion | flops 3227910144 | bytes 12338688 | tf_op jit(solution)/shard_map/dot_general | solution.py:80
  165.1 7.8 %convolution_convert_fusion = bf16[384,1024]{1,0:T(8,128)(2,1)S(1)} fusion(bf16[4096,1024]{1,0:T(8,128)(2,1)} %all-gather.12.cloned.1.call-done, bf16[384,4096]{1,0:T(8,128)(2,1)} %all-gather.8.cloned.1.call-done, f32[4096]{0:T(1024)S(1)} %convert_element_type.46, f32[384]{0:T(512)S(1)} %add_rsqrt_fusion), kind=kOutput, calls=%fused_computation.45 | convolution fusion | flops 3227910144 | bytes 12338688 | tf_op jit(solution)/shard_map/dot_general | solution.py:80
  172.9 30.5 %all-gather.10.cloned.1.call-done = bf16[4096,1024]{1,0:T(8,128)(2,1)} async-done(((bf16[512,1024]{1,0:T(8,128)(2,1)}), bf16[4096,1024]{1,0:T(8,128)(2,1)}) %all-gather.10.cloned.1.call-update) | async-done | bytes 8388624 | tf_op jit(solution)/shard_map/all_gather | solution.py:83
  203.4 7.8 %convolution_convert_fusion.1 = bf16[384,1024]{1,0:T(8,128)(2,1)S(1)} fusion(bf16[4096,1024]{1,0:T(8,128)(2,1)} %all-gather.10.cloned.1.call-done, bf16[384,4096]{1,0:T(8,128)(2,1)} %all-gather.8.cloned.1.call-done, f32[4096]{0:T(1024)S(1)} %convert_element_type.46, f32[384]{0:T(512)S(1)} %add_rsqrt_fusion), kind=kOutput, calls=%fused_computation.46 | convolution fusion | flops 3227910144 | bytes 12338688 | tf_op jit(solution)/shard_map/dot_general | solution.py:80
  214.7 18.7 %gather_fusion = f32[4096,1024]{1,0:T(8,128)} fusion(f32[64,1024]{1,0:T(8,128)S(1)} %bitcast.57, s32[4096]{0:T(1024)S(1)} %broadcast_clamp_fusion), kind=kCustom, calls=%fused_computation | custom fusion | bytes 33570816 | tf_op jit(solution)/shard_map/gather | solution.py:107
  233.4 30.8 %copy.31 = f32[64,64,1024]{1,0,2:T(8,128)} copy(f32[64,64,1024]{2,1,0:T(8,128)} %bitcast.58) | data formatting | bytes 33554432 | tf_op jit(solution)/shard_map/gather | solution.py:107
  271.0 2.7 copy.32
  273.7 16.8 %fusion.24 = f32[6,1024,16]{2,0,1:T(8,128)} fusion(f32[6,64,1024]{1,0,2:T(8,128)} %copy.32, f32[64]{0:T(128)S(1)} %broadcast_subtract_fusion, f32[1024,16]{1,0:T(8,128)S(1)} %copy.30), kind=kOutput, calls=%fused_computation.39 | convolution fusion | flops 76546048 | bytes 2031872 | tf_op jit(solution)/shard_map/sck,bsc->bck/dot_general | solution.py:111
  290.5 2.7 copy.34
  293.6 10.2 %all-gather.1 = f32[8192,16]{0,1:T(8,128)S(1)} all-gather(f32[1024,16]{0,1:T(8,128)S(1)} %get-tuple-element.128), channel_id=3, replica_groups=mesh['ctx'=8,'dp'=4] {'ctx'}, dimensions={0}, use_global_device_ids=true | all-gather | bytes 589824 | tf_op jit(solution)/shard_map/all_gather | solution.py:35
  304.1 9.8 %while.28 = (s32[]{:T(128)}, f32[1024,16]{0,1:T(8,128)S(1)}, s32[]{:T(128)}, f32[8,1024,16]{1,0,2:T(8,128)}, f32[8,1024,16]{1,0,2:T(8,128)S(1)}, /*index=5*/s32[]{:T(128)}, s32[]{:T(128)}) while((s32[]{:T(128)}, f32[1024,16]{0,1:T(8,128)S(1)}, s32[]{:T(128)}, f32[8,1024,16]{1,0,2:T(8,128)}, f32[8,1024,16]{1,0,2:T(8,128)S(1)}, ...), condition=%wide.region_4.5_spmd.clone, body=%wide.region_3.4_spmd.clone.sunk | while | flops 65540 | bytes 524397 | solution.py:47
  314.0 2.7 copy.38
  316.7 56.2 %fusion.3 = f32[1024,6,64]{2,1,0:T(8,128)S(1)} fusion(f32[6,64,1024]{1,0,2:T(8,128)} %copy.32, f32[64,64,1024]{1,0,2:T(8,128)} %copy.31, pred[64,64]{1,0:T(8,128)(4,1)S(1)} %subtract_compare_fusion), kind=kOutput, calls=%fused_computation.10 | convolution fusion | flops 306184192 | bytes 19927040 | tf_op jit(solution)/shard_map/tsc,bsc->btc/dot_general | solution.py:109
  372.9 12.4 %add_bitcast_fusion = f32[6,64,1024]{1,0,2:T(8,128)} fusion(f32[1024,6,64]{2,1,0:T(8,128)S(1)} %fusion.3, f32[6,1024,16]{2,0,1:T(8,128)S(1)} %copy-done.3, f32[1024,16]{1,0:T(8,128)S(1)} %copy-done.9, f32[64]{0:T(128)S(1)} %broadcast_add_fusion, f32[1024,16]{1,0:T(8,128)S(1)} %copy.30), kind=kOutput, calls=%fused_computation.32 | convolution fusion | flops 77987840 | bytes 3670272 | tf_op jit(solution)/shard_map/tck,bck->btc/dot_general | solution.py:132
  385.3 2.8 copy.39
  388.1 3.8 fusion.29
  392.0 63.6 %all-gather.14.cloned.1.call-done = bf16[384,4096]{1,0:T(8,128)(2,1)} async-done(((bf16[384,1024]{1,0:T(8,128)(2,1)}), bf16[384,4096]{1,0:T(8,128)(2,1)}) %all-gather.14.cloned.1.call-update) | async-done | bytes 3145744 | tf_op jit(solution)/shard_map/all_gather | solution.py:135
  455.5 8.7 %add_convert_fusion = bf16[384,1024]{1,0:T(8,128)(2,1)} fusion(bf16[384,1024]{1,0:T(8,128)(2,1)S(1)} %copy-done.8, bf16[384,4096]{1,0:T(8,128)(2,1)} %all-gather.14.cloned.1.call-done, bf16[4096,1024]{1,0:T(8,128)(2,1)} %all-gather.16.cloned.1.call-done), kind=kOutput, calls=%fused_computation.44 | convolution fusion | flops 3222405120 | bytes 13107200 | tf_op jit(solution)/shard_map/dot_general | solution.py:136
  (118 shorter events, 35.6 us)
Async XLA Ops:
  6.5 1.2 copy-start
  6.5 66.6 %copy-start.11 = (f32[1024,16]{0,1:T(8,128)S(1)}, f32[1024,16]{0,1:T(8,128)}, u32[]{:S(2)}) copy-start(f32[1024,16]{0,1:T(8,128)} %param.22) | copy-start | bytes 196612
  6.5 66.6 %copy-start.12 = (f32[1024,16]{0,1:T(8,128)S(1)}, f32[1024,16]{0,1:T(8,128)}, u32[]{:S(2)}) copy-start(f32[1024,16]{0,1:T(8,128)} %param.23) | copy-start | bytes 196612
  6.5 140.1 %all-gather.8.cloned.1.call-start = ((), (), s32[]{:S(2)}) async-start(), calls=%async_computation | async-start | bytes 3932160 | tf_op jit(solution)/shard_map/all_gather | solution.py:71
  10.0 95.0 %copy-start.5 = (bf16[512,1024]{1,0:T(8,128)(2,1)S(1)}, bf16[512,1024]{1,0:T(8,128)(2,1)}, u32[]{:S(2)}) copy-start(bf16[512,1024]{1,0:T(8,128)(2,1)} %param.18) | copy-start | bytes 3145732
  10.0 155.1 %all-gather.12.cloned.1.call-start = ((), (), s32[]{:S(2)}) async-start(), calls=%async_computation.2 | async-start | bytes 9437184 | tf_op jit(solution)/shard_map/all_gather | solution.py:84
  10.7 192.7 %all-gather.10.cloned.1.call-start = ((), (), s32[]{:S(2)}) async-start(), calls=%async_computation.1 | async-start | bytes 9437184 | tf_op jit(solution)/shard_map/all_gather | solution.py:83
  11.5 94.8 %copy-start.15 = (bf16[1024]{0:T(1024)(128)(2,1)S(1)}, bf16[1024]{0:T(1024)(128)(2,1)}, u32[]{:S(2)}) copy-start(bf16[1024]{0:T(1024)(128)(2,1)} %param.17) | copy-start | bytes 6148
  11.5 380.5 %all-gather.16.cloned.1.call-start = ((), (), s32[]{:S(2)}) async-start(), calls=%async_computation.4 | async-start | bytes 9437184 | tf_op jit(solution)/shard_map/all_gather | solution.py:138
  11.5 16.1 %collective-permute-start = (bf16[512,1024]{1,0:T(8,128)(2,1)}, bf16[512,1024]{1,0:T(8,128)(2,1)S(1)}, u32[]{:S(2)}, u32[]{:S(2)}) collective-permute-start(bf16[512,1024]{1,0:T(8,128)(2,1)} %param.18), channel_id=1, source_target_pairs={{0,4},{4,8},{8,12},{12,16},{16,20},{20,24},{24,28},{28,0},{1,5},{5... | collective-permute-start | bytes 3145736 | tf_op jit(solution)/shard_map/ppermute | solution.py:20
  27.6 45.5 %copy-start.6 = (bf16[512,1024]{1,0:T(8,128)(2,1)}, bf16[512,1024]{1,0:T(8,128)(2,1)S(1)}, u32[]{:S(2)}) copy-start(bf16[512,1024]{1,0:T(8,128)(2,1)S(1)} %collective-permute-done) | copy-start | bytes 3145732
  27.6 15.1 %collective-permute-start.1 = (bf16[512,1024]{1,0:T(8,128)(2,1)S(1)}, bf16[512,1024]{1,0:T(8,128)(2,1)S(1)}, u32[]{:S(2)}, u32[]{:S(2)}) collective-permute-start(bf16[512,1024]{1,0:T(8,128)(2,1)S(1)} %collective-permute-done), channel_id=1, source_target_pairs={{0,4},{4,8},{8,12},{12,16},{16,20},{20,24},{24,28},{28,0},{1,5},{5... | collective-permute-start | bytes 3145736 | tf_op jit(solution)/shard_map/ppermute | solution.py:20
  42.8 15.1 %copy-start.7 = (bf16[512,1024]{1,0:T(8,128)(2,1)}, bf16[512,1024]{1,0:T(8,128)(2,1)S(1)}, u32[]{:S(2)}) copy-start(bf16[512,1024]{1,0:T(8,128)(2,1)S(1)} %collective-permute-done.1) | copy-start | bytes 3145732
  42.8 15.1 %collective-permute-start.2 = (bf16[512,1024]{1,0:T(8,128)(2,1)S(1)}, bf16[512,1024]{1,0:T(8,128)(2,1)S(1)}, u32[]{:S(2)}, u32[]{:S(2)}) collective-permute-start(bf16[512,1024]{1,0:T(8,128)(2,1)S(1)} %collective-permute-done.1), channel_id=1, source_target_pairs={{0,4},{4,8},{8,12},{12,16},{16,20},{20,24},{24,28},{28,0},{1,5},{5... | collective-permute-start | bytes 3145736 | tf_op jit(solution)/shard_map/ppermute | solution.py:20
  57.9 15.2 %collective-permute-start.3 = (bf16[512,1024]{1,0:T(8,128)(2,1)S(1)}, bf16[512,1024]{1,0:T(8,128)(2,1)}, u32[]{:S(2)}, u32[]{:S(2)}) collective-permute-start(bf16[512,1024]{1,0:T(8,128)(2,1)S(1)} %collective-permute-done.2), channel_id=1, source_target_pairs={{0,4},{4,8},{8,12},{12,16},{16,20},{20,24},{24,28},{28,0},{1,5},{5... | collective-permute-start | bytes 3145736 | tf_op jit(solution)/shard_map/ppermute | solution.py:20
  57.9 397.6 %all-gather.14.cloned.1.call-start = ((), (), s32[]{:S(2)}) async-start(), calls=%async_computation.3 | async-start | bytes 3932160 | tf_op jit(solution)/shard_map/all_gather | solution.py:135
  73.1 32.9 %collective-permute-start.4 = (bf16[512,1024]{1,0:T(8,128)(2,1)}, bf16[512,1024]{1,0:T(8,128)(2,1)}, u32[]{:S(2)}, u32[]{:S(2)}) collective-permute-start(bf16[512,1024]{1,0:T(8,128)(2,1)} %collective-permute-done.3), channel_id=1, source_target_pairs={{0,4},{4,8},{8,12},{12,16},{16,20},{20,24},{24,28},{28,0},{1,5},{5... | collective-permute-start | bytes 3145736 | tf_op jit(solution)/shard_map/ppermute | solution.py:20
  73.2 46.8 %copy-start.13 = (f32[3,3,1024]{2,1,0:T(4,128)S(1)}, f32[3,3,1024]{2,1,0:T(4,128)}, u32[]{:S(2)}) copy-start(f32[3,3,1024]{2,1,0:T(4,128)} %param.21) | copy-start | bytes 110596
  106.0 34.7 %collective-permute-start.5 = (bf16[512,1024]{1,0:T(8,128)(2,1)}, bf16[512,1024]{1,0:T(8,128)(2,1)S(1)}, u32[]{:S(2)}, u32[]{:S(2)}) collective-permute-start(bf16[512,1024]{1,0:T(8,128)(2,1)} %collective-permute-done.4), channel_id=1, source_target_pairs={{0,4},{4,8},{8,12},{12,16},{16,20},{20,24},{24,28},{28,0},{1,5},{5... | collective-permute-start | bytes 3145736 | tf_op jit(solution)/shard_map/ppermute | solution.py:20
  140.8 15.7 %collective-permute-start.6 = (bf16[512,1024]{1,0:T(8,128)(2,1)S(1)}, bf16[512,1024]{1,0:T(8,128)(2,1)}, u32[]{:S(2)}, u32[]{:S(2)}) collective-permute-start(bf16[512,1024]{1,0:T(8,128)(2,1)S(1)} %collective-permute-done.5), channel_id=1, source_target_pairs={{0,4},{4,8},{8,12},{12,16},{16,20},{20,24},{24,28},{28,0},{1,5},{5... | collective-permute-start | bytes 3145736 | tf_op jit(solution)/shard_map/ppermute | solution.py:20
  146.6 12.4 %copy-start.4 = (bf16[384,4096]{1,0:T(8,128)(2,1)S(1)}, bf16[384,4096]{1,0:T(8,128)(2,1)}, u32[]{:S(2)}) copy-start(bf16[384,4096]{1,0:T(8,128)(2,1)} %all-gather.8.cloned.1.call-done) | copy-start | bytes 9437188
  211.2 55.2 %collective-permute-start.7 = (bf16[2,3072]{1,0:T(2,128)(2,1)S(1)}, bf16[2,3072]{1,0:T(2,128)(2,1)S(1)}, u32[]{:S(2)}, u32[]{:S(2)}) collective-permute-start(bf16[2,3072]{1,0:T(2,128)(2,1)S(1)} %pad_maximum_fusion), channel_id=1, source_target_pairs={{0,4},{4,8},{8,12},{12,16},{16,20},{20,24},{24,28},{1,5},{5,9},{9,... | collective-permute-start | bytes 36872 | tf_op jit(solution)/shard_map/ppermute | solution.py:30
  268.5 2.2 copy-start.2
  273.7 19.5 %copy-start.10 = (f32[6,1024,16]{1,2,0:T(8,128)S(1)}, f32[6,1024,16]{1,2,0:T(8,128)}, u32[]{:S(2)}) copy-start(f32[6,1024,16]{1,2,0:T(8,128)} %custom-call.4) | copy-start | bytes 1179652
  316.7 56.2 %copy-start.3 = (f32[6,1024,16]{2,0,1:T(8,128)S(1)}, f32[6,1024,16]{2,0,1:T(8,128)}, u32[]{:S(2)}) copy-start(f32[6,1024,16]{2,0,1:T(8,128)} %copy.38) | copy-start | bytes 1179652
  316.7 56.2 %copy-start.9 = (f32[1024,16]{1,0:T(8,128)S(1)}, f32[1024,16]{1,0:T(8,128)}, u32[]{:S(2)}) copy-start(f32[1024,16]{1,0:T(8,128)} %copy.47) | copy-start | bytes 196612
  372.9 15.2 %copy-start.14 = (f32[1024]{0:T(1024)S(1)}, f32[1024]{0:T(1024)}, u32[]{:S(2)}) copy-start(f32[1024]{0:T(1024)} %param.24) | copy-start | bytes 12292
  385.3 70.2 %copy-start.8 = (bf16[384,1024]{1,0:T(8,128)(2,1)S(1)}, bf16[384,1024]{1,0:T(8,128)(2,1)}, u32[]{:S(2)}) copy-start(bf16[384,1024]{1,0:T(8,128)(2,1)} %convolution_convert_fusion.3) | copy-start | bytes 2359300
  455.5 8.7 %copy-start.1 = (bf16[512,1024]{1,0:T(8,128)(2,1)S(1)}, bf16[512,1024]{1,0:T(8,128)(2,1)}, u32[]{:S(2)}) copy-start(bf16[512,1024]{1,0:T(8,128)(2,1)} %param.16) | copy-start | bytes 3145732
Sparse Core Ops, SparseCore 0:
  10.1 66.1 all-gather.7
  78.2 67.9 all-gather.11
  148.1 55.2 all-gather.9
  205.1 54.2 all-gather.15
  392.1 63.4 all-gather.13
